TPU v7x, 512 devices: a whole 4x8x8 slice. The times are simulated.
512 devices in a mesh: grp: 16 (over x, z_lo), blk: 32 (over y, z_hi, core).
Axes of the slice: x: 4, y: 8, z: 8 (z_hi: 2, z_lo: 4; z = z_hi * 4 + z_lo), core: 2. Of those that a mesh axis runs over, the one named last changes fastest.
Arguments:
- users: float32 [131072, 256], P(('grp', 'blk')), may hold values from -0.125 to 0.125
- user_momentum: float32 [131072, 256], P(('grp', 'blk')), may hold values from -6 to 6
- items: float32 [8192, 256], P('blk'), may hold values from -0.125 to 0.125
- item_momentum: float32 [8192, 256], P('blk'), may hold values from -6 to 6
- ratings: float32 [131072, 6, 256], P(('grp', 'blk')), may hold values from -6 to 6
- rating_mask: int32 [131072, 6, 256], P(('grp', 'blk')), may hold values 0 or 1
- tile_occupied: int32 [1024, 6, 2], P(('grp', 'blk')), may hold values 0 or 1
- stagger: int32 [16], replicated, may hold values from 0 to 31
Outputs:
- new_users: float32 [131072, 256], P(('grp', 'blk'))
- new_user_momentum: float32 [131072, 256], P(('grp', 'blk'))
- new_items: float32 [8192, 256], P(('blk', 'grp'))
All inputs are finite; a program needn't handle non-finite values. No bound on the sum of `rating_mask` or of `tile_occupied` on one device may be relied on, other than what follows from the above.
Results may differ from a plain program's by a relative error of at most 0.0003.
Values sent between devices are 32-bit elements; how exact they have to be, the bound alone decides.
A program may use at most 64 MiB of HBM per device.

v0:
```python
import jax
import jax.numpy as jnp
from jax import lax
from jax.sharding import PartitionSpec as P

TILE = 128
STEPS = 6
PASSES = 2


momentum_decay = 0.9
shrinkage = 0.05
rate_scale = 0.8


def passed_along(array, axis, by):
    count = lax.axis_size(axis)
    return lax.ppermute(array, axis, [(i, (i + by) % count) for i in range(count)])


def split_up(array, dim, count):
    before, after = (array.shape[:dim], array.shape[dim + 1 :])
    return jnp.moveaxis(array.reshape(*before, count, -1, *after), dim, 0)


def sum_at_owner(array, axis, dim):
    parts = split_up(array, dim, lax.axis_size(axis))
    arrived = lax.all_to_all(parts, axis, split_axis=0, concat_axis=0, tiled=True)
    return arrived.sum(axis=0)


def on_device(
    users, user_momentum, items, item_momentum, ratings, rating_mask, tile_occupied, stagger
):
    highest = lax.Precision.HIGHEST
    cycle_size = lax.axis_size("blk")
    group_count = lax.axis_size("grp")
    offset = stagger[lax.axis_index("grp")]
    held_pair = jnp.stack([items, item_momentum])
    opening = (cycle_size - offset) % cycle_size
    flat_pair = held_pair.reshape(1, -1)
    spread = lax.all_to_all(flat_pair, "blk", split_axis=1, concat_axis=0, tiled=True)
    spread = jnp.roll(spread, opening, axis=0)
    gathered_back = lax.all_to_all(spread, "blk", split_axis=0, concat_axis=1, tiled=True)
    held_pair = gathered_back.reshape(held_pair.shape)
    user_rows = users
    user_mom = user_momentum
    user_count = rating_mask.shape[0]
    item_count = rating_mask.shape[2]
    user_rate = rate_scale / item_count
    item_rate = rate_scale / user_count
    user_tiles = user_count // TILE
    item_tiles = item_count // TILE
    for step in range(STEPS):
        marks = rating_mask[:, step, :].reshape(user_tiles, TILE, item_tiles, TILE)
        tiles = tile_occupied[:, step, :][:, None, :, None]
        weight = (marks * tiles).reshape(user_count, item_count).astype(jnp.float32)
        target = ratings[:, step, :]
        item_rows = held_pair[0]
        item_mom = held_pair[1]
        for repeat in range(PASSES):
            predicted = lax.dot_general(
                user_rows,
                item_rows,
                (((1,), (1,)), ((), ())),
                precision=highest,
                preferred_element_type=jnp.float32,
            )
            residue = weight * (predicted - target)
            user_grad = (
                jnp.dot(residue, item_rows, precision=highest, preferred_element_type=jnp.float32)
                + shrinkage * user_rows
            )
            item_grad = (
                lax.dot_general(
                    residue,
                    user_rows,
                    (((0,), (0,)), ((), ())),
                    precision=highest,
                    preferred_element_type=jnp.float32,
                )
                + shrinkage * item_rows
            )
            user_mom = momentum_decay * user_mom + user_grad
            item_mom = momentum_decay * item_mom + item_grad
            user_rows = user_rows - user_rate * user_mom
            item_rows = item_rows - item_rate * item_mom
        held_pair = jnp.stack([item_rows, item_mom])
        if step + 1 < STEPS:
            held_pair = passed_along(held_pair, "blk", 1)
    final_rows = held_pair[0]
    closing = (offset - (STEPS - 1)) % cycle_size
    flat_rows = final_rows.reshape(1, -1)
    spread_rows = lax.all_to_all(flat_rows, "blk", split_axis=1, concat_axis=0, tiled=True)
    spread_rows = jnp.roll(spread_rows, closing, axis=0)
    returned = lax.all_to_all(spread_rows, "blk", split_axis=0, concat_axis=1, tiled=True)
    final_rows = returned.reshape(final_rows.shape)
    change = final_rows - items
    share = items.shape[0] // group_count
    first = lax.axis_index("grp") * share
    base = lax.dynamic_slice_in_dim(items, first, share, 0)
    owned = sum_at_owner(change, "grp", 0)
    new_items = base + owned / group_count
    return (user_rows, user_mom, new_items)


def solution(mesh):
    in_specs = (
        P(("grp", "blk"), None),
        P(("grp", "blk"), None),
        P("blk", None),
        P("blk", None),
        P(("grp", "blk"), None, None),
        P(("grp", "blk"), None, None),
        P(("grp", "blk"), None, None),
        P(),
    )
    out_specs = (P(("grp", "blk"), None), P(("grp", "blk"), None), P(("blk", "grp"), None))
    return jax.shard_map(
        on_device, mesh=mesh, in_specs=in_specs, out_specs=out_specs, check_vma=False
    )
```

profile of v0, /device:TPU:1, one launch (start us, length us, event | category | flops | bytes accessed | tf_op | source)
XLA Modules:
  0.0 247.3 jit_solution(11751772251238127525)
XLA Ops:
  0.6 1.1 pad_maximum_fusion
  1.7 1.3 all_to_all.47
  3.0 17.2 %all-to-all-start = ((f32[1,32,4096]{2,0,1:T(1,128)}), f32[1,32,4096]{2,0,1:T(1,128)S(1)}, u32[]{:S(2)}, u32[]{:S(2)}) async-start(f32[1,32,4096]{2,0,1:T(1,128)} %all_to_all.47), calls=%async_computation | async-start | bytes 1048576 | tf_op jit(solution)/shard_map/all_to_all | solution.py:42
  20.3 0.6 dynamic_slice.14
  21.5 17.7 %all-to-all-done = f32[1,32,4096]{2,0,1:T(1,128)S(1)} async-done(((f32[1,32,4096]{2,0,1:T(1,128)}), f32[1,32,4096]{2,0,1:T(1,128)S(1)}, u32[]{:S(2)}, u32[]{:S(2)}) %all-to-all-start) | async-done | bytes 524320 | tf_op jit(solution)/shard_map/all_to_all | solution.py:42
  39.7 1.4 all_to_all.50
  41.1 6.2 %all-to-all-start.1 = ((f32[32,1,4096]{2,1,0:T(1,128)}), f32[32,1,4096]{2,1,0:T(1,128)S(1)}, u32[]{:S(2)}, u32[]{:S(2)}) async-start(f32[32,1,4096]{2,1,0:T(1,128)} %all_to_all.50), calls=%async_computation.1 | async-start | bytes 1048576 | tf_op jit(solution)/shard_map/all_to_all | solution.py:44
  48.0 18.3 %all-to-all-done.1 = f32[32,1,4096]{2,1,0:T(1,128)S(1)} async-done(((f32[32,1,4096]{2,1,0:T(1,128)}), f32[32,1,4096]{2,1,0:T(1,128)S(1)}, u32[]{:S(2)}, u32[]{:S(2)}) %all-to-all-start.1) | async-done | bytes 524320 | tf_op jit(solution)/shard_map/all_to_all | solution.py:44
  66.3 1.5 fusion.45
  68.0 0.4 fusion.26
  68.7 0.6 fusion.24
  69.3 0.4 fusion.23
  69.7 0.4 fusion.22
  70.2 0.4 fusion.20
  70.7 6.4 %collective-permute-start = (f32[2,256,256]{2,1,0:T(8,128)S(1)}, f32[2,256,256]{2,1,0:T(8,128)S(1)}, u32[]{:S(2)}, u32[]{:S(2)}) collective-permute-start(f32[2,256,256]{2,1,0:T(8,128)S(1)} %pad_maximum_fusion.1), channel_id=1, source_target_pairs={{0,1},{1,2},{2,3},{3,4},{4,5},{5,6},{6,7},{7,8},{8,9},{9,10},{10,1... | collective-permute-start | bytes 1572872 | tf_op jit(solution)/shard_map/ppermute | solution.py:18
  77.1 0.6 multiply_subtract_fusion.16
  77.7 6.7 %collective-permute-done = f32[2,256,256]{2,1,0:T(8,128)S(1)} collective-permute-done((f32[2,256,256]{2,1,0:T(8,128)S(1)}, f32[2,256,256]{2,1,0:T(8,128)S(1)}, u32[]{:S(2)}, u32[]{:S(2)}) %collective-permute-start) | collective-permute-done | bytes 524320 | tf_op jit(solution)/shard_map/ppermute | solution.py:18
  84.6 0.4 fusion.19
  85.0 0.6 fusion.44
  85.7 0.4 fusion.18
  86.0 0.4 fusion.17
  86.5 0.6 subtract_bitcast_fusion.3
  87.1 8.8 %collective-permute-start.1 = (f32[2,256,256]{2,1,0:T(8,128)S(1)}, f32[2,256,256]{2,1,0:T(8,128)S(1)}, u32[]{:S(2)}, u32[]{:S(2)}) collective-permute-start(f32[2,256,256]{2,1,0:T(8,128)S(1)} %pad_maximum_fusion.2), channel_id=1, source_target_pairs={{0,1},{1,2},{2,3},{3,4},{4,5},{5,6},{6,7},{7,8},{8,9},{9,10},{10,1... | collective-permute-start | bytes 1572872 | tf_op jit(solution)/shard_map/ppermute | solution.py:18
  95.9 0.4 multiply_subtract_fusion.13
  96.3 5.5 %collective-permute-done.1 = f32[2,256,256]{2,1,0:T(8,128)S(1)} collective-permute-done((f32[2,256,256]{2,1,0:T(8,128)S(1)}, f32[2,256,256]{2,1,0:T(8,128)S(1)}, u32[]{:S(2)}, u32[]{:S(2)}) %collective-permute-start.1) | collective-permute-done | bytes 524320 | tf_op jit(solution)/shard_map/ppermute | solution.py:18
  102.0 0.4 fusion.15
  102.4 0.6 fusion.42
  103.0 0.4 fusion.14
  103.4 0.4 fusion.13
  103.8 0.6 subtract_bitcast_fusion.2
  104.5 8.3 %collective-permute-start.2 = (f32[2,256,256]{2,1,0:T(8,128)S(1)}, f32[2,256,256]{2,1,0:T(8,128)S(1)}, u32[]{:S(2)}, u32[]{:S(2)}) collective-permute-start(f32[2,256,256]{2,1,0:T(8,128)S(1)} %pad_maximum_fusion.3), channel_id=1, source_target_pairs={{0,1},{1,2},{2,3},{3,4},{4,5},{5,6},{6,7},{7,8},{8,9},{9,10},{10,1... | collective-permute-start | bytes 1572872 | tf_op jit(solution)/shard_map/ppermute | solution.py:18
  112.8 0.4 multiply_subtract_fusion.10
  113.2 12.0 %collective-permute-done.2 = f32[2,256,256]{2,1,0:T(8,128)S(1)} collective-permute-done((f32[2,256,256]{2,1,0:T(8,128)S(1)}, f32[2,256,256]{2,1,0:T(8,128)S(1)}, u32[]{:S(2)}, u32[]{:S(2)}) %collective-permute-start.2) | collective-permute-done | bytes 524320 | tf_op jit(solution)/shard_map/ppermute | solution.py:18
  125.3 0.4 fusion.11
  125.8 0.6 fusion.40
  126.4 0.4 fusion.10
  126.8 0.4 fusion.9
  127.2 0.6 subtract_bitcast_fusion.1
  127.9 3.9 %collective-permute-start.3 = (f32[2,256,256]{2,1,0:T(8,128)S(1)}, f32[2,256,256]{2,1,0:T(8,128)S(1)}, u32[]{:S(2)}, u32[]{:S(2)}) collective-permute-start(f32[2,256,256]{2,1,0:T(8,128)S(1)} %pad_maximum_fusion.4), channel_id=1, source_target_pairs={{0,1},{1,2},{2,3},{3,4},{4,5},{5,6},{6,7},{7,8},{8,9},{9,10},{10,1... | collective-permute-start | bytes 1572872 | tf_op jit(solution)/shard_map/ppermute | solution.py:18
  131.7 0.4 multiply_subtract_fusion.7
  132.1 16.8 %collective-permute-done.3 = f32[2,256,256]{2,1,0:T(8,128)S(1)} collective-permute-done((f32[2,256,256]{2,1,0:T(8,128)S(1)}, f32[2,256,256]{2,1,0:T(8,128)S(1)}, u32[]{:S(2)}, u32[]{:S(2)}) %collective-permute-start.3) | collective-permute-done | bytes 524320 | tf_op jit(solution)/shard_map/ppermute | solution.py:18
  149.1 0.4 fusion.7
  149.6 0.6 fusion.38
  150.2 0.4 fusion.6
  150.5 0.4 fusion.5
  151.0 0.6 subtract_bitcast_fusion
  151.6 2.1 collective-permute-start.4
  153.8 0.4 multiply_subtract_fusion.4
  154.2 17.7 %collective-permute-done.4 = f32[2,256,256]{2,1,0:T(8,128)S(1)} collective-permute-done((f32[2,256,256]{2,1,0:T(8,128)S(1)}, f32[2,256,256]{2,1,0:T(8,128)S(1)}, u32[]{:S(2)}, u32[]{:S(2)}) %collective-permute-start.4) | collective-permute-done | bytes 524320 | tf_op jit(solution)/shard_map/ppermute | solution.py:18
  172.0 0.4 fusion.3
  172.5 0.6 fusion.36
  173.1 0.4 fusion.2
  173.5 0.4 fusion.1
  173.9 0.6 multiply_subtract_fusion
  174.5 1.0 all_to_all.58
  175.5 20.7 %all-to-all-start.2 = ((f32[1,32,2048]{2,0,1:T(1,128)}), f32[1,32,2048]{2,0,1:T(1,128)S(1)}, u32[]{:S(2)}, u32[]{:S(2)}) async-start(f32[1,32,2048]{2,0,1:T(1,128)} %all_to_all.58), calls=%async_computation.2 | async-start | bytes 524288 | tf_op jit(solution)/shard_map/all_to_all | solution.py:94
  196.9 14.6 %all-to-all-done.2 = f32[1,32,2048]{2,0,1:T(1,128)S(1)} async-done(((f32[1,32,2048]{2,0,1:T(1,128)}), f32[1,32,2048]{2,0,1:T(1,128)S(1)}, u32[]{:S(2)}, u32[]{:S(2)}) %all-to-all-start.2) | async-done | bytes 262176 | tf_op jit(solution)/shard_map/all_to_all | solution.py:94
  211.9 19.2 %all_to_all.64 = f32[32,1,2048]{2,1,0:T(1,128)S(1)} all-to-all(f32[32,1,2048]{2,1,0:T(1,128)S(1)} %all_to_all.55), channel_id=1, replica_groups=mesh['grp'=16,'blk'=32] {'blk'}, dimensions={0} | all-to-all | bytes 524288 | tf_op jit(solution)/shard_map/all_to_all | solution.py:96
  231.2 0.6 reduce.7
  231.9 0.7 sub.172
  232.6 4.1 %all-to-all-start.4 = ((f32[16,16,256]{2,1,0:T(8,128)}), f32[16,16,256]{2,1,0:T(8,128)S(1)}, u32[]{:S(2)}, u32[]{:S(2)}) async-start(f32[16,16,256]{2,1,0:T(8,128)} %bitcast.38), calls=%async_computation.4 | async-start | bytes 524288 | tf_op jit(solution)/shard_map/all_to_all | solution.py:28
  236.7 1.2 multiply_subtract_fusion.1
  237.9 8.7 %all-to-all-done.4 = f32[16,16,256]{2,1,0:T(8,128)S(1)} async-done(((f32[16,16,256]{2,1,0:T(8,128)}), f32[16,16,256]{2,1,0:T(8,128)S(1)}, u32[]{:S(2)}, u32[]{:S(2)}) %all-to-all-start.4) | async-done | bytes 262176 | tf_op jit(solution)/shard_map/all_to_all | solution.py:28
  246.7 0.6 multiply_add_fusion
  (43 shorter events, 3.0 us)
Async XLA Ops:
  0.6 19.6 %copy-start.6 = (s32[16]{0:T(128)S(1)}, s32[16]{0:T(128)}, u32[]{:S(2)}) copy-start(s32[16]{0:T(128)} %param.15) | copy-start | bytes 196
  3.0 36.2 %all-to-all-start = ((f32[1,32,4096]{2,0,1:T(1,128)}), f32[1,32,4096]{2,0,1:T(1,128)S(1)}, u32[]{:S(2)}, u32[]{:S(2)}) async-start(f32[1,32,4096]{2,0,1:T(1,128)} %all_to_all.47), calls=%async_computation | async-start | bytes 1048576 | tf_op jit(solution)/shard_map/all_to_all | solution.py:42
  39.7 7.6 %slice-start = ((f32[256,6,256]{2,0,1:T(8,128)}), f32[256,1,256]{2,0,1:T(8,128)S(1)}, s32[]{:S(2)}) async-start(f32[256,6,256]{2,0,1:T(8,128)} %param.12), calls=%async_computation.5 | async-start | bytes 524288 | tf_op jit(solution)/shard_map/slice | solution.py:58
  39.7 7.7 %copy-start.5 = (s32[2,6,2]{1,2,0:T(2,128)S(1)}, s32[2,6,2]{1,2,0:T(2,128)}, u32[]{:S(2)}) copy-start(s32[2,6,2]{1,2,0:T(2,128)} %param.14) | copy-start | bytes 292
  41.1 6.8 %slice-start.1 = ((s32[256,6,256]{2,0,1:T(8,128)}), s32[256,1,256]{2,0,1:T(8,128)S(1)}, s32[]{:S(2)}) async-start(s32[256,6,256]{2,0,1:T(8,128)} %param.13), calls=%async_computation.6 | async-start | bytes 524288 | tf_op jit(solution)/shard_map/slice | solution.py:55
  41.1 25.2 %all-to-all-start.1 = ((f32[32,1,4096]{2,1,0:T(1,128)}), f32[32,1,4096]{2,1,0:T(1,128)S(1)}, u32[]{:S(2)}, u32[]{:S(2)}) async-start(f32[32,1,4096]{2,1,0:T(1,128)} %all_to_all.50), calls=%async_computation.1 | async-start | bytes 1048576 | tf_op jit(solution)/shard_map/all_to_all | solution.py:44
  47.9 20.1 %copy-start = (f32[256,256]{1,0:T(8,128)S(1)}, f32[256,256]{1,0:T(8,128)}, u32[]{:S(2)}) copy-start(f32[256,256]{1,0:T(8,128)} %param.8) | copy-start | bytes 786436
  67.8 1.0 copy-start.4
  70.7 14.0 %copy-start.1 = (f32[256,6,256]{2,0,1:T(8,128)S(1)}, f32[256,6,256]{2,0,1:T(8,128)}, u32[]{:S(2)}) copy-start(f32[256,6,256]{2,0,1:T(8,128)} %param.12) | copy-start | bytes 4718596
  70.7 14.0 %copy-start.2 = (s32[256,6,256]{2,0,1:T(8,128)S(1)}, s32[256,6,256]{2,0,1:T(8,128)}, u32[]{:S(2)}) copy-start(s32[256,6,256]{2,0,1:T(8,128)} %param.13) | copy-start | bytes 4718596
  70.7 13.8 %collective-permute-start = (f32[2,256,256]{2,1,0:T(8,128)S(1)}, f32[2,256,256]{2,1,0:T(8,128)S(1)}, u32[]{:S(2)}, u32[]{:S(2)}) collective-permute-start(f32[2,256,256]{2,1,0:T(8,128)S(1)} %pad_maximum_fusion.1), channel_id=1, source_target_pairs={{0,1},{1,2},{2,3},{3,4},{4,5},{5,6},{6,7},{7,8},{8,9},{9,10},{10,1... | collective-permute-start | bytes 1572872 | tf_op jit(solution)/shard_map/ppermute | solution.py:18
  87.1 14.7 %collective-permute-start.1 = (f32[2,256,256]{2,1,0:T(8,128)S(1)}, f32[2,256,256]{2,1,0:T(8,128)S(1)}, u32[]{:S(2)}, u32[]{:S(2)}) collective-permute-start(f32[2,256,256]{2,1,0:T(8,128)S(1)} %pad_maximum_fusion.2), channel_id=1, source_target_pairs={{0,1},{1,2},{2,3},{3,4},{4,5},{5,6},{6,7},{7,8},{8,9},{9,10},{10,1... | collective-permute-start | bytes 1572872 | tf_op jit(solution)/shard_map/ppermute | solution.py:18
  104.5 20.7 %collective-permute-start.2 = (f32[2,256,256]{2,1,0:T(8,128)S(1)}, f32[2,256,256]{2,1,0:T(8,128)S(1)}, u32[]{:S(2)}, u32[]{:S(2)}) collective-permute-start(f32[2,256,256]{2,1,0:T(8,128)S(1)} %pad_maximum_fusion.3), channel_id=1, source_target_pairs={{0,1},{1,2},{2,3},{3,4},{4,5},{5,6},{6,7},{7,8},{8,9},{9,10},{10,1... | collective-permute-start | bytes 1572872 | tf_op jit(solution)/shard_map/ppermute | solution.py:18
  127.9 21.1 %collective-permute-start.3 = (f32[2,256,256]{2,1,0:T(8,128)S(1)}, f32[2,256,256]{2,1,0:T(8,128)S(1)}, u32[]{:S(2)}, u32[]{:S(2)}) collective-permute-start(f32[2,256,256]{2,1,0:T(8,128)S(1)} %pad_maximum_fusion.4), channel_id=1, source_target_pairs={{0,1},{1,2},{2,3},{3,4},{4,5},{5,6},{6,7},{7,8},{8,9},{9,10},{10,1... | collective-permute-start | bytes 1572872 | tf_op jit(solution)/shard_map/ppermute | solution.py:18
  151.6 20.3 %collective-permute-start.4 = (f32[2,256,256]{2,1,0:T(8,128)S(1)}, f32[2,256,256]{2,1,0:T(8,128)S(1)}, u32[]{:S(2)}, u32[]{:S(2)}) collective-permute-start(f32[2,256,256]{2,1,0:T(8,128)S(1)} %pad_maximum_fusion.5), channel_id=1, source_target_pairs={{0,1},{1,2},{2,3},{3,4},{4,5},{5,6},{6,7},{7,8},{8,9},{9,10},{10,1... | collective-permute-start | bytes 1572872 | tf_op jit(solution)/shard_map/ppermute | solution.py:18
  175.5 36.1 %all-to-all-start.2 = ((f32[1,32,2048]{2,0,1:T(1,128)}), f32[1,32,2048]{2,0,1:T(1,128)S(1)}, u32[]{:S(2)}, u32[]{:S(2)}) async-start(f32[1,32,2048]{2,0,1:T(1,128)} %all_to_all.58), calls=%async_computation.2 | async-start | bytes 524288 | tf_op jit(solution)/shard_map/all_to_all | solution.py:94
  196.9 34.9 %copy-start.3 = (f32[256,256]{1,0:T(8,128)S(1)}, f32[256,256]{1,0:T(8,128)}, u32[]{:S(2)}) copy-start(f32[256,256]{1,0:T(8,128)} %param.10) | copy-start | bytes 786436
  232.6 14.0 %all-to-all-start.4 = ((f32[16,16,256]{2,1,0:T(8,128)}), f32[16,16,256]{2,1,0:T(8,128)S(1)}, u32[]{:S(2)}, u32[]{:S(2)}) async-start(f32[16,16,256]{2,1,0:T(8,128)} %bitcast.38), calls=%async_computation.4 | async-start | bytes 524288 | tf_op jit(solution)/shard_map/all_to_all | solution.py:28
where the time goes:
time: 248 us; the launch traced here: 247 us
  waiting for transfers between devices  118 us (48%)
  starting transfers between devices  77.7 us (31%)
  blocking collectives  19.2 us (8%)
  matrix products  17.9 us (7%)
  local copies, waits for them, and re-layouts  6.77 us (3%)
  other arithmetic  4.96 us (2%)
  between operations  2.63 us (1%)
    ppermute x5, waiting for transfers between devices, passed_along(): lax.ppermute(array, axis, [(i, (i + by) % count) for i in range(count)])  58.8 us
    ppermute x5, starting transfers between devices, passed_along(): lax.ppermute(array, axis, [(i, (i + by) % count) for i in range(count)])  29.4 us
    all_to_all x1, starting transfers between devices, on_device(): lax.all_to_all(flat_rows, 'blk', split_axis=1, concat_axis=0, tiled=True)  20.7 us
    all_to_all x1, blocking collectives, on_device(): lax.all_to_all(spread_rows, 'blk', split_axis=0, concat_axis=1, tiled=True)  19.2 us
    all_to_all x1, waiting for transfers between devices, on_device(): lax.all_to_all(spread, 'blk', split_axis=0, concat_axis=1, tiled=True)  18.3 us
    all_to_all x1, waiting for transfers between devices, on_device(): lax.all_to_all(flat_pair, 'blk', split_axis=1, concat_axis=0, tiled=True)  17.7 us
    all_to_all x1, starting transfers between devices, on_device(): lax.all_to_all(flat_pair, 'blk', split_axis=1, concat_axis=0, tiled=True)  17.2 us
    all_to_all x1, waiting for transfers between devices, on_device(): lax.all_to_all(flat_rows, 'blk', split_axis=1, concat_axis=0, tiled=True)  14.6 us
  transfers between devices with their start and end apart: 9, of which 9 were waited for; matrix products, arithmetic and copies ran while one was open for 2% of the time, Pallas kernels for 0%

commit v1 on v0

v1 whole, which is shorter than its diff:
```python
import functools

import jax
import jax.numpy as jnp
from jax import lax
from jax.experimental import pallas as pl
from jax.experimental.pallas import tpu as pltpu
from jax.sharding import PartitionSpec as P

TILE = 128
STEPS = 6
PASSES = 2
GEOM = (4, 4, 8)
YC = 2
LANES = 128

momentum_decay = 0.9
shrinkage = 0.05
rate_scale = 0.8

MESH = pl.DeviceIdType.MESH
f32 = jnp.float32
bf16 = jnp.bfloat16


def split2(a):
    hi = a.astype(bf16)
    return hi, (a - hi.astype(f32)).astype(bf16)


def dot3(a, b, dims):
    def one(p, q):
        return lax.dot_general(p, q, (dims, ((), ())), preferred_element_type=f32)

    return one(a[0], b[0]) + (one(a[0], b[1]) + one(a[1], b[0]))


def kernel(
    stag, tiles, users, umom, items, imom, ratings, mask,
    out_u, out_p, out_i,
    own, got, outbox, hold, raw_m, rat, wgt,
    fin, c1_out, c1_in, c2_out, c2_in, c3_out, c3_in,
    load_sem, s1, r1, s2, r2, ring_s, ring_r, sc, rc,
):
    nx, nl, ny = GEOM
    nz = 2 * nl
    ng, nb = nx * nl, ny * 4
    rank = out_u.shape[1]
    halves = rank // LANES
    n_items = own.shape[1]
    n_users = out_u.shape[0]
    prow = got.shape[2]
    g = lax.axis_index("grp")
    b = lax.axis_index("blk")
    x, y, z, c = g // nl, b // 4, (b // 2) % 2 * nl + g % nl, b % 2

    def dev(xx, yy, zz, cc):
        return (xx * nl + zz % nl, (yy * 2 + zz // nl) * 2 + cc)

    def piece_of(xx, yy, zz, cc):
        return ((xx * nl + zz % nl) * 2 + cc) * YC + yy % YC

    def part(ref, p):
        row = pl.multiple_of(p // halves * prow, prow)
        col = pl.multiple_of(p % halves * LANES, LANES)
        return ref.at[:, pl.ds(row, prow), pl.ds(col, LANES)]

    loads = []
    for i, (src, dst) in enumerate(
        (
            (items, own.at[0]),
            (imom, own.at[1]),
            (ratings, rat),
            (mask, raw_m),
            (users, out_u),
            (umom, out_p),
        )
    ):
        copy = pltpu.make_async_copy(src, dst, load_sem.at[i])
        copy.start()
        loads.append(copy)

    def offsets(xs, cs):
        for dz in range(nl):
            zoff = dz if 2 * dz < nl else dz - nl
            if 2 * dz == nl:
                zoff = dz * (1 - 2 * (xs % 2))
            for dy in range(YC):
                yoff = dy
                if 2 * dy == YC:
                    yoff = dy * (1 - 2 * cs)
                yield dz, dy, zoff, yoff

    def second(sign):
        for dx in range(nx):
            for dc in range(2):
                other = ((x + dx) % nx, (c + dc) % 2)
                sx, sc_ = other if sign > 0 else (x, c)
                for dz, dy, zoff, yoff in offsets(sx, sc_):
                    at = (
                        other[0],
                        (y + sign * yoff + ny) % ny,
                        (z + sign * zoff + nz) % nz,
                        other[1],
                    )
                    yield (dx == 0 and dz == 0), (dx + dc + dz + dy == 0), at

    barrier = pltpu.get_barrier_semaphore()
    count = 0
    greet = [(g, (b + d) % nb) for d in range(1, nb)]
    greet += [dev(x, yy, nz - 1 - z, cc) for yy in range(ny) for cc in range(2)]
    greet += [dev(*at) for near, _, at in second(1) if not near]
    greet += [((g + d) % ng, b) for d in range(1, ng)]
    for who in greet:
        pl.semaphore_signal(barrier, inc=1, device_id=who, device_id_type=MESH)
        count += 1
    loads[0].wait()
    loads[1].wait()
    pl.semaphore_wait(barrier, count)

    mine = piece_of(x, y, z, c)
    for dy in range(ny):
        for flip in range(2):
            for dc in range(2):
                if dy + flip + dc == 0:
                    continue
                yy, zz, cc = (y + dy) % ny, (nz - 1 - z if flip else z), (c + dc) % 2
                pltpu.make_async_remote_copy(
                    src_ref=part(own, piece_of(x, yy, zz, cc)),
                    dst_ref=got.at[b],
                    send_sem=s1,
                    recv_sem=r1,
                    device_id=dev(x, yy, zz, cc),
                    device_id_type=MESH,
                ).start()
    got[b] = part(own, mine)[...]

    loads[2].wait()
    loads[3].wait()
    for s in range(STEPS):
        for ut in range(n_users // TILE):
            for it in range(n_items // TILE):
                ur, ir = pl.ds(ut * TILE, TILE), pl.ds(it * TILE, TILE)
                wgt[s, ur, ir] = (raw_m[s, ur, ir] * tiles[s, ut, it]).astype(f32)
    loads[4].wait()
    loads[5].wait()

    several = got.at[pl.ds(0, nb - 1)]
    pltpu.make_async_copy(several, several, r1).wait()

    outs = list(second(-1))
    k = 0
    sends = []
    for _, self_, at in outs:
        gd, bd = dev(*at)
        at_block = (bd + stag[gd]) % nb
        if self_:
            part(hold.at[0], mine)[...] = got[at_block]
        else:
            outbox[k] = got[at_block]
            sends.append((k, (gd, bd)))
            k += 1
    for k, who in sends:
        pltpu.make_async_remote_copy(
            src_ref=outbox.at[k],
            dst_ref=part(hold.at[0], mine),
            send_sem=s2,
            recv_sem=r2,
            device_id=who,
            device_id_type=MESH,
        ).start()
    sent = outbox.at[pl.ds(0, len(sends))]
    pltpu.make_async_copy(sent, sent, r2).wait()

    def onward(s):
        return pltpu.make_async_remote_copy(
            src_ref=hold.at[s],
            dst_ref=hold.at[s + 1],
            send_sem=ring_s.at[s],
            recv_sem=ring_r.at[s],
            device_id=(g, (b + 1) % nb),
            device_id_type=MESH,
        )

    user_rate = rate_scale / n_items
    item_rate = rate_scale / n_users

    def step(s, carry):
        @pl.when(s > 0)
        def _():
            onward(s - 1).wait_recv()

        for _ in range(PASSES):
            u, v = out_u[...], hold[s, 0]
            us, vs = split2(u), split2(v)
            pred = dot3(us, vs, ((1,), (1,)))
            res = split2(wgt[s] * (pred - rat[s]))
            ugrad = dot3(res, vs, ((1,), (0,))) + shrinkage * u
            igrad = dot3(res, us, ((0,), (0,))) + shrinkage * v
            p = momentum_decay * out_p[...] + ugrad
            m = momentum_decay * hold[s, 1] + igrad
            out_p[...] = p
            out_u[...] = u - user_rate * p
            hold[s, 1] = m
            hold[s, 0] = v - item_rate * m

        @pl.when(s < STEPS - 1)
        def _():
            onward(s).start()

        return carry

    lax.fori_loop(0, STEPS, step, 0)

    per = n_items // ng
    for h in range(halves):
        fin[pl.ds(h * n_items, n_items), :] = hold[STEPS - 1, 0, :, pl.ds(h * LANES, LANES)]
    for t in range(nb):
        r, h = t % per, t // per
        c1_out[t] = fin[pl.ds(h * n_items + r, ng, stride=per), :]
    for d in range(1, nb):
        t = (b + d) % nb
        pltpu.make_async_remote_copy(
            src_ref=c1_out.at[t],
            dst_ref=c1_in.at[b],
            send_sem=sc.at[0],
            recv_sem=rc.at[0],
            device_id=(g, t),
            device_id_type=MESH,
        ).start()
    c1_in[b] = c1_out[b]
    some = c1_in.at[pl.ds(0, nb - 1)]
    pltpu.make_async_copy(some, some, rc.at[0]).wait()
    shift = nb - stag[g] + STEPS - 1
    for j in range(nb):
        c2_out[pl.ds(j, ng, stride=nb), :] = c1_in[(j + shift) % nb]
    for d in range(1, ng):
        t = (g + d) % ng
        pltpu.make_async_remote_copy(
            src_ref=c2_out.at[pl.ds(pl.multiple_of(t * nb, nb), nb)],
            dst_ref=c2_in.at[g],
            send_sem=sc.at[1],
            recv_sem=rc.at[1],
            device_id=(t, b),
            device_id_type=MESH,
        ).start()
    c2_in[g] = c2_out[pl.ds(pl.multiple_of(g * nb, nb), nb), :]
    some2 = c2_in.at[pl.ds(0, ng - 1)]
    pltpu.make_async_copy(some2, some2, rc.at[1]).wait()
    total = c2_in[0]
    for i in range(1, ng):
        total = total + c2_in[i]
    total = total / ng
    for j in range(nb):
        c3_out[j] = total[j : j + 1]
    for d in range(1, nb):
        t = (b + d) % nb
        pltpu.make_async_remote_copy(
            src_ref=c3_out.at[t],
            dst_ref=c3_in.at[b],
            send_sem=sc.at[2],
            recv_sem=rc.at[2],
            device_id=(g, t),
            device_id_type=MESH,
        ).start()
    c3_in[b] = c3_out[b]

    pltpu.make_async_copy(several, several, s1).wait()
    pltpu.make_async_copy(sent, sent, s2).wait()
    for s in range(STEPS - 1):
        onward(s).wait_send()
    pltpu.make_async_copy(some, some, sc.at[0]).wait()
    pltpu.make_async_copy(some2, some2, sc.at[1]).wait()
    some3 = c3_in.at[pl.ds(0, nb - 1)]
    pltpu.make_async_copy(some3, some3, sc.at[2]).wait()
    pltpu.make_async_copy(some3, some3, rc.at[2]).wait()
    for t in range(nb):
        r, h = t % per, t // per
        out_i[pl.ds(r, 1), pl.ds(h * LANES, LANES)] = c3_in[t]


def on_device(
    users, user_momentum, items, item_momentum, ratings, rating_mask, tile_occupied, stagger
):
    nx, nl, ny = GEOM
    ng, nb = nx * nl, ny * 4
    n_users, rank = users.shape
    n_items = items.shape[0]
    pieces = ng * 2 * YC
    prow = n_items * (rank // LANES) // pieces
    vm = pl.BlockSpec(memory_space=pltpu.VMEM)
    sm = pl.BlockSpec(memory_space=pltpu.SMEM)
    hbm = pl.BlockSpec(memory_space=pl.ANY)
    dma = pltpu.SemaphoreType.DMA
    return pl.pallas_call(
        kernel,
        out_shape=(
            jax.ShapeDtypeStruct(users.shape, f32),
            jax.ShapeDtypeStruct(users.shape, f32),
            jax.ShapeDtypeStruct((n_items // ng, rank), f32),
        ),
        in_specs=[sm, sm] + [hbm] * 6,
        out_specs=(vm, vm, vm),
        scratch_shapes=[
            pltpu.VMEM((2, n_items, rank), f32),
            pltpu.VMEM((nb, 2, prow, LANES), f32),
            pltpu.VMEM((pieces, 2, prow, LANES), f32),
            pltpu.VMEM((STEPS, 2, n_items, rank), f32),
            pltpu.VMEM((STEPS, n_users, n_items), jnp.int32),
            pltpu.VMEM((STEPS, n_users, n_items), f32),
            pltpu.VMEM((STEPS, n_users, n_items), f32),
            pltpu.VMEM((n_items * (rank // LANES), LANES), f32),
            pltpu.VMEM((nb, ng, LANES), f32),
            pltpu.VMEM((nb, ng, LANES), f32),
            pltpu.VMEM((ng * nb, LANES), f32),
            pltpu.VMEM((ng, nb, LANES), f32),
            pltpu.VMEM((nb, 1, LANES), f32),
            pltpu.VMEM((nb, 1, LANES), f32),
            dma((6,)),
            dma,
            dma,
            dma,
            dma,
            dma((STEPS - 1,)),
            dma((STEPS - 1,)),
            dma((3,)),
            dma((3,)),
        ],
        compiler_params=pltpu.CompilerParams(
            collective_id=0, has_side_effects=True, vmem_limit_bytes=60 * 2**20
        ),
        name="window",
    )(
        stagger,
        jnp.transpose(tile_occupied, (1, 0, 2)),
        users,
        user_momentum,
        items,
        item_momentum,
        jnp.transpose(ratings, (1, 0, 2)),
        jnp.transpose(rating_mask, (1, 0, 2)),
    )


def solution(mesh):
    in_specs = (
        P(("grp", "blk"), None),
        P(("grp", "blk"), None),
        P("blk", None),
        P("blk", None),
        P(("grp", "blk"), None, None),
        P(("grp", "blk"), None, None),
        P(("grp", "blk"), None, None),
        P(),
    )
    out_specs = (P(("grp", "blk"), None), P(("grp", "blk"), None), P(("blk", "grp"), None))
    return jax.shard_map(
        on_device, mesh=mesh, in_specs=in_specs, out_specs=out_specs, check_vma=False
    )
```

time: 248 us -> 139 us (0.56)
  Pallas kernels: 0 us -> 132 us
  waiting for transfers between devices: 118 us -> 0 us
  starting transfers between devices: 77.7 us -> 0 us
  blocking collectives: 19.2 us -> 0 us
  matrix products: 17.9 us -> 0 us
  other arithmetic: 4.96 us -> 0 us
    pallas_call x0 -> x1, Pallas kernels: none -> 132 us  [on_device(): pl.pallas_call(kernel, out_shape=(jax.ShapeDtypeStruct(users.shape, f32),...]
    all_to_all x4 -> x0, waiting for transfers between devices: 59.3 us -> none  [the longest x1 18.3 us: on_device(): lax.all_to_all(spread, 'blk', split_axis=0, concat_axis=1, tiled=True)]
    ppermute x5 -> x0, waiting for transfers between devices: 58.8 us -> none  [passed_along(): lax.ppermute(array, axis, [(i, (i + by) % count) for i in range(count)])]
    all_to_all x4 -> x0, starting transfers between devices: 48.2 us -> none  [the longest x1 20.7 us: on_device(): lax.all_to_all(flat_rows, 'blk', split_axis=1, concat_axis=0, tiled=True)]
    ppermute x5 -> x0, starting transfers between devices: 29.4 us -> none  [passed_along(): lax.ppermute(array, axis, [(i, (i + by) % count) for i in range(count)])]
    all_to_all x1 -> x0, blocking collectives: 19.2 us -> none  [on_device(): lax.all_to_all(spread_rows, 'blk', split_axis=0, concat_axis=1, tiled=True)]
    dot_general x36 -> x0, matrix products: 17.9 us -> none  [the longest x12 6.85 us: on_device(): lax.dot_general(residue, user_rows, (((0,), (0,)), ((), ())), precision=h...]
    unnamed x18 -> x4, local copies, waits for them, and re-layouts: 0.95 us -> 6.02 us
  transfers between devices with their start and end apart: 9 -> 0, of which waited for: 9 -> 0; matrix products, arithmetic and copies ran while one was open for 2% -> 0% of each run, Pallas kernels for 0% -> 0%
where the time goes in v1:
time: 139 us
  Pallas kernels  132 us (95%)
  local copies, waits for them, and re-layouts  6.02 us (4%)
    pallas_call x1, Pallas kernels, on_device(): pl.pallas_call(kernel, out_shape=(jax.ShapeDtypeStruct(users.shape, f32),...  132 us
    unnamed x4, local copies, waits for them, and re-layouts  6.02 us

profile of v1, /device:TPU:1, one launch (start us, length us, event | category | flops | bytes accessed | tf_op | source)
XLA Modules:
  0.0 138.6 jit_solution(9899359222121859651)
XLA Ops:
  0.6 1.4 copy.11
  2.0 131.9 %window.1 = (f32[256,256]{1,0:T(8,128)}, f32[256,256]{1,0:T(8,128)}, f32[16,256]{1,0:T(8,128)}) custom-call(s32[16]{0:T(128)} %stag.1, s32[6,2,2]{2,1,0:T(2,128)} %bitcast.5, f32[256,256]{1,0:T(8,128)} %users.1, f32[256,256]{1,0:T(8,128)} %umom.1, f32[256,256]{1,0:T(8,128)} %items.1, f32[256,256]{1,0:T(8,128)} %imom.1, f32[6,256,256]{2,1,0:T(8,128)} %bitcast.3, ...), custom_call_target="tpu_custom_call" | custom-call | tf_op jit(solution)/shard_map/window/pallas_call | solution.py:295
  133.9 1.7 %copy.15 = f32[256,256]{1,0:T(8,128)} copy(f32[256,256]{1,0:T(8,128)} %get-tuple-element.6) | data formatting | bytes 524288
  135.6 1.7 %copy.16 = f32[256,256]{1,0:T(8,128)} copy(f32[256,256]{1,0:T(8,128)} %get-tuple-element.7) | data formatting | bytes 524288
  137.3 1.3 copy.17

commit v2 on v1

v2 whole, which is shorter than its diff:
```python
import functools

import jax
import jax.numpy as jnp
from jax import lax
from jax.experimental import pallas as pl
from jax.experimental.pallas import tpu as pltpu
from jax.sharding import PartitionSpec as P

TILE = 128
STEPS = 6
PASSES = 2
GEOM = (4, 4, 8)
YC_OPEN = 4
YC_CLOSE = 2
LANES = 128

momentum_decay = 0.9
shrinkage = 0.05
rate_scale = 0.8

MESH = pl.DeviceIdType.MESH
f32 = jnp.float32
bf16 = jnp.bfloat16


def split2(a):
    hi = a.astype(bf16)
    return hi, (a - hi.astype(f32)).astype(bf16)


def dot3(a, b, dims):
    def one(p, q):
        return lax.dot_general(p, q, (dims, ((), ())), preferred_element_type=f32)

    return one(a[0], b[0]) + (one(a[0], b[1]) + one(a[1], b[0]))


def kernel(
    stag, tiles, users, umom, items, imom, ratings, mask,
    out_u, out_p, out_i,
    own, got, outbox, hold, raw_m, rat, wgt,
    c1_in, c2_out, c2_in,
    load_sem, s1, r1, s2, r2, ring_s, ring_r, sc, rc,
):
    nx, nl, ny = GEOM
    nz = 2 * nl
    ng, nb = nx * nl, ny * 4
    rank = out_u.shape[1]
    halves = rank // LANES
    n_items = own.shape[1]
    n_users = out_u.shape[0]
    planes, prow = got.shape[1], got.shape[2]
    g = lax.axis_index("grp")
    b = lax.axis_index("blk")
    x, y, z, c = g // nl, b // 4, (b // 2) % 2 * nl + g % nl, b % 2

    def dev(xx, yy, zz, cc):
        return (xx * nl + zz % nl, (yy * 2 + zz // nl) * 2 + cc)

    def rows_cols(xx, yy, zz, cc):
        row = ((xx * nl + zz % nl) * 2 + cc) * prow
        col = yy % halves * LANES
        return pl.ds(pl.multiple_of(row, prow), prow), pl.ds(pl.multiple_of(col, LANES), LANES)

    def part(ref, at):
        plane = at[1] % YC_OPEN // halves * planes
        return ref.at[(pl.ds(plane, planes), *rows_cols(*at))]

    loads = []
    for i, (src, dst) in enumerate(
        (
            (items, own.at[0]),
            (imom, own.at[1]),
            (ratings, rat),
            (mask, raw_m),
            (users, out_u),
            (umom, out_p),
        )
    ):
        copy = pltpu.make_async_copy(src, dst, load_sem.at[i])
        copy.start()
        loads.append(copy)

    def pairs(classes, sign):
        found = [((x, y, z, 1 - c), True)]
        for cc in (1, 0):
            for dx in range(nx):
                xx = (x + dx) % nx
                hx, hc = (xx, cc) if sign > 0 else (x, c)
                for dz in range(nl):
                    zoff = dz if 2 * dz < nl else dz - nl
                    if 2 * dz == nl:
                        zoff = dz * (1 - 2 * (hx % 2))
                    for dy in range(classes):
                        yoff = dy if 2 * dy < classes else dy - classes
                        if 2 * dy == classes:
                            yoff = dy * (1 - 2 * hc)
                        if dx + dz + dy:
                            yy = (y + sign * yoff + ny) % ny
                            zz = (z + sign * zoff + nz) % nz
                            found.append(((xx, yy, zz, cc), dx + dz == 0))
        return found

    for gg in range(ng):
        c1_in[gg] = jnp.zeros(c1_in.shape[1:], f32)

    barrier = pltpu.get_barrier_semaphore()
    greet = [(g, (b + d) % nb) for d in range(1, nb)]
    greet += [dev(x, yy, nz - 1 - z, cc) for yy in range(ny) for cc in range(2)]
    greet += [dev(*at) for at, near in pairs(YC_OPEN, 1) if not near]
    greet += [dev(*at) for at, near in pairs(YC_CLOSE, -1) if not near]
    for who in greet:
        pl.semaphore_signal(barrier, inc=1, device_id=who, device_id_type=MESH)
    loads[0].wait()
    loads[1].wait()
    pl.semaphore_wait(barrier, len(greet))

    me = (x, y, z, c)
    for dy in sorted(range(ny), key=lambda d: -min(d, ny - d)):
        for flip in range(2):
            for dc in range(2):
                if dy + flip + dc == 0:
                    continue
                at = (x, (y + dy) % ny, (nz - 1 - z if flip else z), (c + dc) % 2)
                pltpu.make_async_remote_copy(
                    src_ref=part(own, at),
                    dst_ref=got.at[b],
                    send_sem=s1,
                    recv_sem=r1,
                    device_id=dev(*at),
                    device_id_type=MESH,
                ).start()
    got[b] = part(own, me)[...]

    for copy in loads[2:]:
        copy.wait()
    for s in range(STEPS):
        for ut in range(n_users // TILE):
            for it in range(n_items // TILE):
                ur, ir = pl.ds(ut * TILE, TILE), pl.ds(it * TILE, TILE)
                wgt[s, ur, ir] = (raw_m[s, ur, ir] * tiles[ut, it, s]).astype(f32)

    several = got.at[pl.ds(0, nb - 1)]
    pltpu.make_async_copy(several, several, r1).wait()

    part(hold.at[0], me)[...] = got[(b + stag[g]) % nb]
    outs = [dev(*at) for at, _ in pairs(YC_OPEN, -1)]
    for k, (gd, bd) in enumerate(outs):
        outbox[k] = got[(bd + stag[gd]) % nb]
    for k, who in enumerate(outs):
        pltpu.make_async_remote_copy(
            src_ref=outbox.at[k],
            dst_ref=part(hold.at[0], me),
            send_sem=s2,
            recv_sem=r2,
            device_id=who,
            device_id_type=MESH,
        ).start()
    sent = outbox.at[pl.ds(0, len(outs))]
    pltpu.make_async_copy(sent, sent, r2).wait()

    def onward(s):
        return pltpu.make_async_remote_copy(
            src_ref=hold.at[s],
            dst_ref=hold.at[s + 1],
            send_sem=ring_s.at[s],
            recv_sem=ring_r.at[s],
            device_id=(g, (b + 1) % nb),
            device_id_type=MESH,
        )

    user_rate = rate_scale / n_items
    item_rate = rate_scale / n_users

    def step(s, carry):
        @pl.when(s > 0)
        def _():
            onward(s - 1).wait_recv()

        for _ in range(PASSES):
            u, v = out_u[...], hold[s, 0]
            us, vs = split2(u), split2(v)
            pred = dot3(us, vs, ((1,), (1,)))
            res = split2(wgt[s] * (pred - rat[s]))
            ugrad = dot3(res, vs, ((1,), (0,))) + shrinkage * u
            igrad = dot3(res, us, ((0,), (0,))) + shrinkage * v
            p = momentum_decay * out_p[...] + ugrad
            m = momentum_decay * hold[s, 1] + igrad
            out_p[...] = p
            out_u[...] = u - user_rate * p
            hold[s, 1] = m
            hold[s, 0] = v - item_rate * m

        @pl.when(s < STEPS - 1)
        def _():
            onward(s).start()

        return carry

    lax.fori_loop(0, STEPS, step, 0)

    last = hold.at[STEPS - 1, 0]
    for at, _ in pairs(YC_CLOSE, 1):
        pltpu.make_async_remote_copy(
            src_ref=last.at[rows_cols(*at)],
            dst_ref=c1_in.at[g, b],
            send_sem=sc.at[0],
            recv_sem=rc.at[0],
            device_id=dev(*at),
            device_id_type=MESH,
        ).start()
    c1_in[g, b] = last[rows_cols(*me)]
    pieces = ng * 2 * YC_CLOSE
    some = outbox.at[pl.ds(0, (pieces - 1) // planes)] if planes == 1 else None
    pltpu.make_async_copy(some, some, rc.at[0]).wait()
    shifts = [nb - stag[gg] + STEPS - 1 for gg in range(ng)]
    for j in range(nb):
        total = c1_in[0, (j + shifts[0]) % nb]
        for gg in range(1, ng):
            total = total + c1_in[gg, (j + shifts[gg]) % nb]
        c2_out[j] = total * (1 / ng)
    for d in sorted(range(1, nb), key=lambda d: -min(d, nb - d)):
        t = (b + d) % nb
        pltpu.make_async_remote_copy(
            src_ref=c2_out.at[t],
            dst_ref=c2_in.at[b],
            send_sem=sc.at[1],
            recv_sem=rc.at[1],
            device_id=(g, t),
            device_id_type=MESH,
        ).start()
    c2_in[b] = c2_out[b]

    pltpu.make_async_copy(several, several, s1).wait()
    pltpu.make_async_copy(sent, sent, s2).wait()
    for s in range(STEPS - 1):
        onward(s).wait_send()
    pltpu.make_async_copy(some, some, sc.at[0]).wait()
    some2 = c2_in.at[pl.ds(0, nb - 1)]
    pltpu.make_async_copy(some2, some2, sc.at[1]).wait()
    pltpu.make_async_copy(some2, some2, rc.at[1]).wait()
    for cc in range(2):
        for h in range(halves):
            held = [c2_in[(yy * 2 + zh) * 2 + cc] for yy in range(h, ny, halves) for zh in range(2)]
            out_i[pl.ds(cc * prow, prow), pl.ds(h * LANES, LANES)] = sum(held[1:], held[0])


def copy_out(*refs):
    n = len(refs) // 2
    for src, dst in zip(refs[:n], refs[n:]):
        dst[...] = src[...]


def on_device(
    users, user_momentum, items, item_momentum, ratings, rating_mask, tile_occupied, stagger
):
    nx, nl, ny = GEOM
    ng, nb = nx * nl, ny * 4
    n_users, rank = users.shape
    n_items = items.shape[0]
    pieces = ng * 2 * YC_OPEN
    planes = 4 // YC_OPEN
    prow = n_items // (ng * 2)
    vm = pl.BlockSpec(memory_space=pltpu.VMEM)
    sm = pl.BlockSpec(memory_space=pltpu.SMEM)
    hbm = pl.BlockSpec(memory_space=pl.ANY)
    dma = pltpu.SemaphoreType.DMA
    results = pl.pallas_call(
        kernel,
        out_shape=(
            jax.ShapeDtypeStruct(users.shape, f32),
            jax.ShapeDtypeStruct(users.shape, f32),
            jax.ShapeDtypeStruct((n_items // ng, rank), f32),
        ),
        in_specs=[sm, sm] + [hbm] * 6,
        out_specs=(vm, vm, vm),
        scratch_shapes=[
            pltpu.VMEM((2, n_items, rank), f32),
            pltpu.VMEM((nb, planes, prow, LANES), f32),
            pltpu.VMEM((pieces, planes, prow, LANES), f32),
            pltpu.VMEM((STEPS, 2, n_items, rank), f32),
            pltpu.VMEM((STEPS, n_users, n_items), jnp.int32),
            pltpu.VMEM((STEPS, n_users, n_items), f32),
            pltpu.VMEM((STEPS, n_users, n_items), f32),
            pltpu.VMEM((ng, nb, prow, LANES), f32),
            pltpu.VMEM((nb, prow, LANES), f32),
            pltpu.VMEM((nb, prow, LANES), f32),
            dma((6,)),
            dma,
            dma,
            dma,
            dma,
            dma((STEPS - 1,)),
            dma((STEPS - 1,)),
            dma((2,)),
            dma((2,)),
        ],
        compiler_params=pltpu.CompilerParams(
            collective_id=0, has_side_effects=True, vmem_limit_bytes=60 * 2**20
        ),
        name="window",
    )(
        stagger,
        jnp.transpose(tile_occupied, (0, 2, 1)),
        users,
        user_momentum,
        items,
        item_momentum,
        jnp.transpose(ratings, (1, 0, 2)),
        jnp.transpose(rating_mask, (1, 0, 2)),
    )
    return pl.pallas_call(
        copy_out,
        out_shape=tuple(jax.ShapeDtypeStruct(r.shape, r.dtype) for r in results),
        in_specs=[vm] * 3,
        out_specs=(vm,) * 3,
        name="results",
    )(*results)


def solution(mesh):
    in_specs = (
        P(("grp", "blk"), None),
        P(("grp", "blk"), None),
        P("blk", None),
        P("blk", None),
        P(("grp", "blk"), None, None),
        P(("grp", "blk"), None, None),
        P(("grp", "blk"), None, None),
        P(),
    )
    out_specs = (P(("grp", "blk"), None), P(("grp", "blk"), None), P(("blk", "grp"), None))
    return jax.shard_map(
        on_device, mesh=mesh, in_specs=in_specs, out_specs=out_specs, check_vma=False
    )
```

time: 139 us -> 126 us (0.906)
  Pallas kernels: 132 us -> 125 us
  local copies, waits for them, and re-layouts: 6.02 us -> 0 us
    pallas_call x1, Pallas kernels: 132 us -> 123 us  [on_device(): pl.pallas_call(kernel, out_shape=(jax.ShapeDtypeStruct(users.shape, f32),...]
    unnamed x4 -> x0, local copies, waits for them, and re-layouts: 6.02 us -> none
    pallas_call x0 -> x1, Pallas kernels: none -> 1.84 us  [on_device(): pl.pallas_call(copy_out, out_shape=tuple((jax.ShapeDtypeStruct(r.shape, r...]
where the time goes in v2:
time: 126 us
  Pallas kernels  125 us (99%)
    pallas_call x1, Pallas kernels, on_device(): pl.pallas_call(kernel, out_shape=(jax.ShapeDtypeStruct(users.shape, f32),...  123 us

profile of v2, /device:TPU:1, one launch (start us, length us, event | category | flops | bytes accessed | tf_op | source)
XLA Modules:
  0.0 125.9 jit_solution(871276448293473561)
XLA Ops:
  0.6 123.5 %window.1 = (f32[256,256]{1,0:T(8,128)}, f32[256,256]{1,0:T(8,128)}, f32[16,256]{1,0:T(8,128)}) custom-call(s32[16]{0:T(128)} %stag.1, s32[2,2,6]{2,1,0:T(2,128)} %bitcast.5, f32[256,256]{1,0:T(8,128)} %users.1, f32[256,256]{1,0:T(8,128)} %umom.1, f32[256,256]{1,0:T(8,128)} %items.1, f32[256,256]{1,0:T(8,128)} %imom.1, f32[6,256,256]{2,1,0:T(8,128)} %bitcast.3, ...), custom_call_target="tpu_custom_call" | custom-call | tf_op jit(solution)/shard_map/window/pallas_call | solution.py:269
  124.1 1.8 %results.1 = (f32[256,256]{1,0:T(8,128)}, f32[256,256]{1,0:T(8,128)}, f32[16,256]{1,0:T(8,128)}) custom-call(f32[256,256]{1,0:T(8,128)} %get-tuple-element.6.refs_0_, f32[256,256]{1,0:T(8,128)} %get-tuple-element.7.refs_1_, f32[16,256]{1,0:T(8,128)} %get-tuple-element.8.refs_2_), custom_call_target="tpu_custom_call" | custom-call | tf_op jit(solution)/shard_map/results/pallas_call | solution.py:313

commit v3 on v2

--- a/solution.py
+++ b/solution.py
@@ -40,7 +40,7 @@
     stag, tiles, users, umom, items, imom, ratings, mask,
     out_u, out_p, out_i,
     own, got, outbox, hold, raw_m, rat, wgt,
-    c1_in, c2_out, c2_in,
+    c1_in, c2_out, c2_in, tally,
     load_sem, s1, r1, s2, r2, ring_s, ring_r, sc, rc,
 ):
     nx, nl, ny = GEOM
@@ -91,11 +91,11 @@
                 for dz in range(nl):
                     zoff = dz if 2 * dz < nl else dz - nl
                     if 2 * dz == nl:
-                        zoff = dz * (1 - 2 * (hx % 2))
+                        zoff = dz * (1 - 2 * hc)
                     for dy in range(classes):
                         yoff = dy if 2 * dy < classes else dy - classes
                         if 2 * dy == classes:
-                            yoff = dy * (1 - 2 * hc)
+                            yoff = dy * (1 - 2 * ((hx + hc) % 2))
                         if dx + dz + dy:
                             yy = (y + sign * yoff + ny) % ny
                             zz = (z + sign * zoff + nz) % nz
@@ -211,8 +211,7 @@
             device_id_type=MESH,
         ).start()
     c1_in[g, b] = last[rows_cols(*me)]
-    pieces = ng * 2 * YC_CLOSE
-    some = outbox.at[pl.ds(0, (pieces - 1) // planes)] if planes == 1 else None
+    some = tally.at[pl.ds(0, ng * 2 * YC_CLOSE - 1)]
     pltpu.make_async_copy(some, some, rc.at[0]).wait()
     shifts = [nb - stag[gg] + STEPS - 1 for gg in range(ng)]
     for j in range(nb):
@@ -286,6 +285,7 @@
             pltpu.VMEM((ng, nb, prow, LANES), f32),
             pltpu.VMEM((nb, prow, LANES), f32),
             pltpu.VMEM((nb, prow, LANES), f32),
+            pltpu.VMEM((ng * 2 * YC_CLOSE, prow, LANES), f32),
             dma((6,)),
             dma,
             dma,

time: 126 us -> 120 us (0.952)
  Pallas kernels: 125 us -> 119 us
    pallas_call x1, Pallas kernels: 123 us -> 117 us  [on_device(): pl.pallas_call(kernel, out_shape=(jax.ShapeDtypeStruct(users.shape, f32),...]
where the time goes in v3:
time: 120 us
  Pallas kernels  119 us (99%)
    pallas_call x1, Pallas kernels, on_device(): pl.pallas_call(kernel, out_shape=(jax.ShapeDtypeStruct(users.shape, f32),...  117 us

profile of v3, /device:TPU:1, one launch (start us, length us, event | category | flops | bytes accessed | tf_op | source)
XLA Modules:
  0.0 119.6 jit_solution(10192310805001178874)
XLA Ops:
  0.6 117.1 %window.1 = (f32[256,256]{1,0:T(8,128)}, f32[256,256]{1,0:T(8,128)}, f32[16,256]{1,0:T(8,128)}) custom-call(s32[16]{0:T(128)} %stag.1, s32[2,2,6]{2,1,0:T(2,128)} %bitcast.5, f32[256,256]{1,0:T(8,128)} %users.1, f32[256,256]{1,0:T(8,128)} %umom.1, f32[256,256]{1,0:T(8,128)} %items.1, f32[256,256]{1,0:T(8,128)} %imom.1, f32[6,256,256]{2,1,0:T(8,128)} %bitcast.3, ...), custom_call_target="tpu_custom_call" | custom-call | tf_op jit(solution)/shard_map/window/pallas_call | solution.py:268
  117.7 1.8 %results.1 = (f32[256,256]{1,0:T(8,128)}, f32[256,256]{1,0:T(8,128)}, f32[16,256]{1,0:T(8,128)}) custom-call(f32[256,256]{1,0:T(8,128)} %get-tuple-element.6.refs_0_, f32[256,256]{1,0:T(8,128)} %get-tuple-element.7.refs_1_, f32[16,256]{1,0:T(8,128)} %get-tuple-element.8.refs_2_), custom_call_target="tpu_custom_call" | custom-call | tf_op jit(solution)/shard_map/results/pallas_call | solution.py:313

commit v4 on v3

--- a/solution.py
+++ b/solution.py
@@ -40,16 +40,15 @@
     stag, tiles, users, umom, items, imom, ratings, mask,
     out_u, out_p, out_i,
     own, got, outbox, hold, raw_m, rat, wgt,
-    c1_in, c2_out, c2_in, tally,
+    user, c1_in, c2_out, c2_in, tally,
     load_sem, s1, r1, s2, r2, ring_s, ring_r, sc, rc,
 ):
     nx, nl, ny = GEOM
     nz = 2 * nl
     ng, nb = nx * nl, ny * 4
-    rank = out_u.shape[1]
+    n_users, rank = user.shape[1:]
     halves = rank // LANES
     n_items = own.shape[1]
-    n_users = out_u.shape[0]
     planes, prow = got.shape[1], got.shape[2]
     g = lax.axis_index("grp")
     b = lax.axis_index("blk")
@@ -74,8 +73,8 @@
             (imom, own.at[1]),
             (ratings, rat),
             (mask, raw_m),
-            (users, out_u),
-            (umom, out_p),
+            (users, user.at[0]),
+            (umom, user.at[1]),
         )
     ):
         copy = pltpu.make_async_copy(src, dst, load_sem.at[i])
@@ -109,7 +108,6 @@
     greet = [(g, (b + d) % nb) for d in range(1, nb)]
     greet += [dev(x, yy, nz - 1 - z, cc) for yy in range(ny) for cc in range(2)]
     greet += [dev(*at) for at, near in pairs(YC_OPEN, 1) if not near]
-    greet += [dev(*at) for at, near in pairs(YC_CLOSE, -1) if not near]
     for who in greet:
         pl.semaphore_signal(barrier, inc=1, device_id=who, device_id_type=MESH)
     loads[0].wait()
@@ -173,64 +171,87 @@
     user_rate = rate_scale / n_items
     item_rate = rate_scale / n_users
 
+    last = hold.at[STEPS - 1, 0]
+
+    def give():
+        for at, _ in pairs(YC_CLOSE, 1):
+            pltpu.make_async_remote_copy(
+                src_ref=last.at[rows_cols(*at)],
+                dst_ref=c1_in.at[g, b],
+                send_sem=sc.at[0],
+                recv_sem=rc.at[0],
+                device_id=dev(*at),
+                device_id_type=MESH,
+            ).start()
+
     def step(s, carry):
         @pl.when(s > 0)
         def _():
             onward(s - 1).wait_recv()
 
-        for _ in range(PASSES):
-            u, v = out_u[...], hold[s, 0]
+        for again in range(PASSES):
+            u, v = user[0], hold[s, 0]
             us, vs = split2(u), split2(v)
             pred = dot3(us, vs, ((1,), (1,)))
             res = split2(wgt[s] * (pred - rat[s]))
-            ugrad = dot3(res, vs, ((1,), (0,))) + shrinkage * u
             igrad = dot3(res, us, ((0,), (0,))) + shrinkage * v
-            p = momentum_decay * out_p[...] + ugrad
             m = momentum_decay * hold[s, 1] + igrad
-            out_p[...] = p
-            out_u[...] = u - user_rate * p
             hold[s, 1] = m
             hold[s, 0] = v - item_rate * m
-
-        @pl.when(s < STEPS - 1)
-        def _():
-            onward(s).start()
+            if again == PASSES - 1:
+
+                @pl.when(s < STEPS - 1)
+                def _():
+                    onward(s).start()
+
+                @pl.when(s == STEPS - 1)
+                def _():
+                    give()
+
+            ugrad = dot3(res, vs, ((1,), (0,))) + shrinkage * u
+            p = momentum_decay * user[1] + ugrad
+            user[1] = p
+            user[0] = u - user_rate * p
 
         return carry
 
     lax.fori_loop(0, STEPS, step, 0)
-
-    last = hold.at[STEPS - 1, 0]
-    for at, _ in pairs(YC_CLOSE, 1):
-        pltpu.make_async_remote_copy(
-            src_ref=last.at[rows_cols(*at)],
-            dst_ref=c1_in.at[g, b],
-            send_sem=sc.at[0],
-            recv_sem=rc.at[0],
-            device_id=dev(*at),
-            device_id_type=MESH,
-        ).start()
+    stores = []
+    for i, dst in enumerate((out_u, out_p)):
+        copy = pltpu.make_async_copy(user.at[i], dst, load_sem.at[i])
+        copy.start()
+        stores.append(copy)
     c1_in[g, b] = last[rows_cols(*me)]
     some = tally.at[pl.ds(0, ng * 2 * YC_CLOSE - 1)]
     pltpu.make_async_copy(some, some, rc.at[0]).wait()
     shifts = [nb - stag[gg] + STEPS - 1 for gg in range(ng)]
-    for j in range(nb):
+
+    def block_sum(j):
         total = c1_in[0, (j + shifts[0]) % nb]
         for gg in range(1, ng):
             total = total + c1_in[gg, (j + shifts[gg]) % nb]
-        c2_out[j] = total * (1 / ng)
-    for d in sorted(range(1, nb), key=lambda d: -min(d, nb - d)):
-        t = (b + d) % nb
-        pltpu.make_async_remote_copy(
-            src_ref=c2_out.at[t],
-            dst_ref=c2_in.at[b],
-            send_sem=sc.at[1],
-            recv_sem=rc.at[1],
-            device_id=(g, t),
-            device_id_type=MESH,
-        ).start()
-    c2_in[b] = c2_out[b]
-
+        return total * (1 / ng)
+
+    waiting = []
+    for d in [*sorted(range(1, nb), key=lambda d: -min(d, nb - d)), 0, 0, 0]:
+        if len(waiting) == 3 or d == 0:
+            t = waiting.pop(0)
+            pltpu.make_async_remote_copy(
+                src_ref=c2_out.at[t],
+                dst_ref=c2_in.at[b],
+                send_sem=sc.at[1],
+                recv_sem=rc.at[1],
+                device_id=(g, t),
+                device_id_type=MESH,
+            ).start()
+        if d:
+            j = (b + d) % nb
+            waiting.append(j)
+            c2_out[j] = block_sum(j)
+    c2_in[b] = block_sum(b)
+
+    for copy in stores:
+        copy.wait()
     pltpu.make_async_copy(several, several, s1).wait()
     pltpu.make_async_copy(sent, sent, s2).wait()
     for s in range(STEPS - 1):
@@ -246,9 +267,17 @@
 
 
 def copy_out(*refs):
-    n = len(refs) // 2
-    for src, dst in zip(refs[:n], refs[n:]):
-        dst[...] = src[...]
+    n = len(refs) // 3
+    sources, results, held, sem = refs[:n], refs[n : 2 * n], refs[2 * n : 3 * n], refs[-1]
+    ins = [pltpu.make_async_copy(r, h, sem.at[i]) for i, (r, h) in enumerate(zip(sources, held))]
+    outs = [pltpu.make_async_copy(h, r, sem.at[n + i]) for i, (h, r) in enumerate(zip(held, results))]
+    for copy in ins:
+        copy.start()
+    for come, go in zip(ins, outs):
+        come.wait()
+        go.start()
+    for copy in outs:
+        copy.wait()
 
 
 def on_device(
@@ -273,7 +302,7 @@
             jax.ShapeDtypeStruct((n_items // ng, rank), f32),
         ),
         in_specs=[sm, sm] + [hbm] * 6,
-        out_specs=(vm, vm, vm),
+        out_specs=(hbm, hbm, vm),
         scratch_shapes=[
             pltpu.VMEM((2, n_items, rank), f32),
             pltpu.VMEM((nb, planes, prow, LANES), f32),
@@ -282,6 +311,7 @@
             pltpu.VMEM((STEPS, n_users, n_items), jnp.int32),
             pltpu.VMEM((STEPS, n_users, n_items), f32),
             pltpu.VMEM((STEPS, n_users, n_items), f32),
+            pltpu.VMEM((2, n_users, rank), f32),
             pltpu.VMEM((ng, nb, prow, LANES), f32),
             pltpu.VMEM((nb, prow, LANES), f32),
             pltpu.VMEM((nb, prow, LANES), f32),
@@ -313,8 +343,10 @@
     return pl.pallas_call(
         copy_out,
         out_shape=tuple(jax.ShapeDtypeStruct(r.shape, r.dtype) for r in results),
-        in_specs=[vm] * 3,
-        out_specs=(vm,) * 3,
+        in_specs=[hbm] * 3,
+        out_specs=(hbm,) * 3,
+        scratch_shapes=[*(pltpu.VMEM(r.shape, r.dtype) for r in results), dma((6,))],
+        compiler_params=pltpu.CompilerParams(vmem_limit_bytes=60 * 2**20),
         name="results",
     )(*results)
 

time: 120 us -> 119 us (level)
  no operation moved by 1% of the time
where the time goes in v4:
time: 119 us
  Pallas kernels  118 us (99%)
    pallas_call x1, Pallas kernels, on_device(): pl.pallas_call(kernel, out_shape=(jax.ShapeDtypeStruct(users.shape, f32),...  116 us

profile of v4, /device:TPU:1, one launch (start us, length us, event | category | flops | bytes accessed | tf_op | source)
XLA Modules:
  0.0 118.6 jit_solution(15642921651730127785)
XLA Ops:
  0.6 116.2 %window.1 = (f32[256,256]{1,0:T(8,128)}, f32[256,256]{1,0:T(8,128)}, f32[16,256]{1,0:T(8,128)}) custom-call(s32[16]{0:T(128)} %stag.1, s32[2,2,6]{2,1,0:T(2,128)} %bitcast.5, f32[256,256]{1,0:T(8,128)} %users.1, f32[256,256]{1,0:T(8,128)} %umom.1, f32[256,256]{1,0:T(8,128)} %items.1, f32[256,256]{1,0:T(8,128)} %imom.1, f32[6,256,256]{2,1,0:T(8,128)} %bitcast.3, ...), custom_call_target="tpu_custom_call" | custom-call | tf_op jit(solution)/shard_map/window/pallas_call | solution.py:297
  116.9 1.8 %results.1 = (f32[256,256]{1,0:T(8,128)}, f32[256,256]{1,0:T(8,128)}, f32[16,256]{1,0:T(8,128)}) custom-call(f32[256,256]{1,0:T(8,128)} %get-tuple-element.6.refs_0_, f32[256,256]{1,0:T(8,128)} %get-tuple-element.7.refs_1_, f32[16,256]{1,0:T(8,128)} %get-tuple-element.8.refs_2_), custom_call_target="tpu_custom_call" | custom-call | tf_op jit(solution)/shard_map/results/pallas_call | solution.py:343
